TPU v7x, 32 devices: a whole 2x2x4 slice. The times are simulated.
32 devices in a mesh: slot: 2 (over x), tile: 4 (over z), obs: 4 (over y, core).
Axes of the slice: x: 2, y: 2, z: 4, core: 2. Of those that a mesh axis runs over, the one named last changes fastest.
Arguments:
- forcing: float32 [2, 128, 32, 512], P('slot', None, 'tile', 'obs'), may hold values from -6 to 6
- winds: float32 [2, 2, 32, 512], P(None, 'slot', 'tile', 'obs'), may hold values from -0.2 to 0.2
- mixing: float32 [128, 128], replicated, may hold values from -0.12 to 0.12
- observation_columns: int32 [4, 2, 8192], P(None, 'slot', ('tile', 'obs')), may hold values from 0 to 1023
- obs_weights: float32 [4, 2, 8192], P(None, 'slot', ('tile', 'obs')), may hold values from 0.05 to 0.5
- obs_counts: int32 [2, 16, 4], P('slot', ('tile', 'obs')), may hold values from 16 to 128, as said below
- jacobian: float32 [2, 4, 128, 128], P('slot', 'obs'), may hold values from -0.5 to 0.5
Outputs:
- states: float32 [2, 128, 32, 512], P('slot', None, 'tile', 'obs')
- radiances: float32 [2, 128, 8192], P('slot', None, ('tile', 'obs'))
Inputs may be any that keep to these rules, and one draw needn't show every extreme that they name: `obs_counts`: every block of 128 rows has its live rows first; in every slot and every tile one owner's blocks are full from every source.
All inputs are finite; a program needn't handle non-finite values.
Results may differ from a plain program's by a relative error of at most 0.0001.
Values sent between devices are 32-bit elements; how exact they have to be, the bound alone decides.
A program may use at most 64 MiB of HBM per device.

v0:
```python
import jax
import jax.numpy as jnp
from jax import lax
from jax.sharding import PartitionSpec as P

STEPS = 4


mixing_rate = 0.15


def padded_2(block, sides, width):
    for axis, dim in sides:
        count = lax.axis_size(axis)
        forward = [(i, i + 1) for i in range(count - 1)]
        forward.append((count - 1, 0))
        backward = [(target, source) for source, target in forward]
        low = lax.ppermute(
            lax.slice_in_dim(block, block.shape[dim] - width, None, axis=dim), axis, forward
        )
        high = lax.ppermute(lax.slice_in_dim(block, 0, width, axis=dim), axis, backward)
        block = jnp.concatenate([low, block, high], axis=dim)
    return block


def passed_along(x, axis, by):
    size = lax.axis_size(axis)
    pairs = [(i, i + by) for i in range(size) if 0 <= i + by < size]
    return lax.ppermute(x, axis, pairs)


def advance_slot(padded, eastward_rate, northward_rate, mixing):
    centre = padded[:, 1:-1, 1:-1]
    eastern = padded[:, 2:, 1:-1]
    western = padded[:, :-2, 1:-1]
    northern = padded[:, 1:-1, 2:]
    southern = padded[:, 1:-1, :-2]
    shifted_state = (
        centre + eastward_rate * (eastern - western) + northward_rate * (northern - southern)
    )
    shifted_state = shifted_state + mixing_rate * (
        eastern + western + northern + southern - 4.0 * centre
    )
    return shifted_state + jnp.einsum(
        "mn,nlk->mlk", mixing, shifted_state, precision=lax.Precision.HIGHEST
    )


def local(forcing, winds, mixing, observation_columns, obs_weights, obs_counts, jacobian):
    source = forcing[0]
    current = source
    rates = winds[:, 0]
    rounds = lax.axis_size("slot") - 1
    width_x = current.shape[1]
    width_y = current.shape[2]
    broad_rates = padded_2(rates, (("tile", 1), ("obs", 2)), STEPS)
    for round_index in range(rounds):
        padded = padded_2(current, (("tile", 1), ("obs", 2)), STEPS)
        for step in range(STEPS):
            margin = STEPS - step - 1
            lower = step + 1
            window = broad_rates[
                :, lower : lower + width_x + 2 * margin, lower : lower + width_y + 2 * margin
            ]
            padded = advance_slot(padded, window[0], window[1], mixing)
        current = padded
        current = passed_along(current, "slot", 1) + source
    levels = current.shape[0]
    flat = current.reshape(levels, width_x * width_y)
    cells = observation_columns[:, 0]
    weights = obs_weights[:, 0]
    profile = weights[0] * jnp.take(flat, cells[0], axis=1)
    for corner in range(1, 4):
        profile = profile + weights[corner] * jnp.take(flat, cells[corner], axis=1)
    owners = obs_counts.shape[2]
    capacity = cells.shape[1] // owners
    live = (jnp.arange(capacity, dtype=jnp.int32)[None, :] < obs_counts[0, 0][:, None]).astype(
        jnp.float32
    )
    profile = profile.reshape(levels, owners, capacity) * live[None]
    table = jacobian[0, 0]
    radiance = jnp.einsum(
        "cv,vsk->csk",
        table,
        lax.all_to_all(profile, "obs", split_axis=1, concat_axis=1, tiled=True),
        precision=lax.Precision.HIGHEST,
    )
    return (current[None], radiance.reshape(1, table.shape[0], owners * capacity))


def solution(mesh):
    return jax.shard_map(
        local,
        mesh=mesh,
        in_specs=(
            P("slot", None, "tile", "obs"),
            P(None, "slot", "tile", "obs"),
            P(),
            P(None, "slot", ("tile", "obs")),
            P(None, "slot", ("tile", "obs")),
            P("slot", ("tile", "obs"), None),
            P("slot", "obs", None, None),
        ),
        out_specs=(P("slot", None, "tile", "obs"), P("slot", None, ("tile", "obs"))),
        check_vma=False,
    )
```

profile of v0, /device:TPU:1, one launch (start us, length us, event | category | flops | bytes accessed | tf_op | source)
XLA Modules:
  0.0 65.2 jit_solution(1980320158361133783)
XLA Ops:
  0.7 1.3 %copy.9 = f32[1,128,8,128]{1,3,2,0:T(8,128)S(1)} copy(f32[1,128,8,128]{3,2,1,0:T(8,128)} %param.9) | data formatting | bytes 1048576 | tf_op args[0]
  2.0 2.2 %collective-permute-start = (f32[128,4,128]{0,2,1:T(8,128)S(1)}, f32[128,4,128]{0,2,1:T(8,128)S(1)}, u32[]{:S(2)}, u32[]{:S(2)}) collective-permute-start(f32[128,4,128]{0,2,1:T(8,128)S(1)} %get-tuple-element.7), channel_id=1, source_target_pairs={{0,4},{4,8},{8,12},{12,0},{1,5},{5,9},{9,13},{13,1},{2,6},{6,10},{... | collective-permute-start | bytes 786440 | tf_op jit(solution)/shard_map/ppermute | solution.py:18
  4.2 2.1 %collective-permute-start.1 = (f32[128,4,128]{0,2,1:T(8,128)S(1)}, f32[128,4,128]{0,2,1:T(8,128)S(1)}, u32[]{:S(2)}, u32[]{:S(2)}) collective-permute-start(f32[128,4,128]{0,2,1:T(8,128)S(1)} %get-tuple-element.8), channel_id=1, source_target_pairs={{4,0},{8,4},{12,8},{0,12},{5,1},{9,5},{13,9},{1,13},{6,2},{10,6},{... | collective-permute-start | bytes 786440 | tf_op jit(solution)/shard_map/ppermute | solution.py:21
  6.3 3.3 %collective-permute-start.5 = (f32[2,4,128]{2,1,0:T(4,128)S(1)}, f32[2,4,128]{2,1,0:T(4,128)S(1)}, u32[]{:S(2)}, u32[]{:S(2)}) collective-permute-start(f32[2,4,128]{2,1,0:T(4,128)S(1)} %get-tuple-element.28), channel_id=1, source_target_pairs={{4,0},{8,4},{12,8},{0,12},{5,1},{9,5},{13,9},{1,13},{6,2},{10,6},{... | collective-permute-start | bytes 12296 | tf_op jit(solution)/shard_map/ppermute | solution.py:21
  9.7 8.0 %collective-permute-done.4 = f32[2,4,128]{2,1,0:T(4,128)S(1)} collective-permute-done((f32[2,4,128]{2,1,0:T(4,128)S(1)}, f32[2,4,128]{2,1,0:T(4,128)S(1)}, u32[]{:S(2)}, u32[]{:S(2)}) %collective-permute-start.4) | collective-permute-done | bytes 4128 | tf_op jit(solution)/shard_map/ppermute | solution.py:18
  17.8 2.7 %collective-permute-start.6 = (f32[2,16,4]{2,1,0:T(8,128)S(1)}, f32[2,16,4]{2,1,0:T(8,128)S(1)}, u32[]{:S(2)}, u32[]{:S(2)}) collective-permute-start(f32[2,16,4]{2,1,0:T(8,128)S(1)} %get-tuple-element.15), channel_id=1, source_target_pairs={{0,1},{1,2},{2,3},{3,0},{4,5},{5,6},{6,7},{7,4},{8,9},{9,10},{10,1... | collective-permute-start | bytes 1544 | tf_op jit(solution)/shard_map/ppermute | solution.py:18
  20.5 0.9 %collective-permute-done.6 = f32[2,16,4]{2,1,0:T(8,128)S(1)} collective-permute-done((f32[2,16,4]{2,1,0:T(8,128)S(1)}, f32[2,16,4]{2,1,0:T(8,128)S(1)}, u32[]{:S(2)}, u32[]{:S(2)}) %collective-permute-start.6) | collective-permute-done | bytes 544 | tf_op jit(solution)/shard_map/ppermute | solution.py:18
  21.3 2.3 %collective-permute-done.7 = f32[2,16,4]{2,1,0:T(8,128)S(1)} collective-permute-done((f32[2,16,4]{2,1,0:T(8,128)S(1)}, f32[2,16,4]{2,1,0:T(8,128)S(1)}, u32[]{:S(2)}, u32[]{:S(2)}) %collective-permute-start.7) | collective-permute-done | bytes 544 | tf_op jit(solution)/shard_map/ppermute | solution.py:21
  25.2 2.2 %collective-permute-done.3 = f32[128,16,4]{0,2,1:T(4,128)S(1)} collective-permute-done((f32[128,16,4]{0,2,1:T(4,128)S(1)}, f32[128,16,4]{0,2,1:T(4,128)S(1)}, u32[]{:S(2)}, u32[]{:S(2)}) %collective-permute-start.3) | collective-permute-done | bytes 32800 | tf_op jit(solution)/shard_map/ppermute | solution.py:21
  27.5 2.6 %fusion = f32[128,14,134]{0,2,1:T(8,128)S(1)} fusion(f32[128,16,136]{0,2,1:T(8,128)S(1)} %pad_maximum_fusion, f32[14,134]{1,0:T(8,128)S(1)} %get-tuple-element.14, f32[14,134]{1,0:T(8,128)S(1)} %get-tuple-element.13, f32[128,128]{1,0:T(8,128)S(1)} %copy-done), kind=kOutput, calls=%fused_computation.5 | convolution fusion | flops 375320064 | bytes 10840064 | tf_op jit(solution)/shard_map/mn,nlk->mlk/dot_general | solution.py:44
  30.1 2.2 %fusion.1 = f32[128,12,132]{0,2,1:T(8,128)S(1)} fusion(f32[128,14,134]{0,2,1:T(8,128)S(1)} %fusion, f32[12,132]{1,0:T(8,128)S(1)} %get-tuple-element.12, f32[12,132]{1,0:T(8,128)S(1)} %get-tuple-element.11, f32[128,128]{1,0:T(8,128)S(1)} %copy-done), kind=kOutput, calls=%fused_computation.7 | convolution fusion | flops 316901376 | bytes 9297920 | tf_op jit(solution)/shard_map/mn,nlk->mlk/dot_general | solution.py:44
  32.3 1.9 %fusion.2 = f32[128,10,130]{0,2,1:T(8,128)S(1)} fusion(f32[128,12,132]{0,2,1:T(8,128)S(1)} %fusion.1, f32[10,130]{1,0:T(8,128)S(1)} %get-tuple-element.10, f32[10,130]{1,0:T(8,128)S(1)} %get-tuple-element.9, f32[128,128]{1,0:T(8,128)S(1)} %copy-done), kind=kOutput, calls=%fused_computation.9 | convolution fusion | flops 260083200 | bytes 7759872 | tf_op jit(solution)/shard_map/mn,nlk->mlk/dot_general | solution.py:44
  34.2 1.5 %fusion.3 = f32[128,8,128]{0,2,1:T(8,128)S(1)} fusion(f32[128,10,130]{0,2,1:T(8,128)S(1)} %fusion.2, f32[8,128]{1,0:T(8,128)S(1)} %get-tuple-element.26, f32[8,128]{1,0:T(8,128)S(1)} %get-tuple-element.25, f32[128,128]{1,0:T(8,128)S(1)} %copy-done), kind=kOutput, calls=%fused_computation.11 | convolution fusion | flops 204865536 | bytes 5849088 | tf_op jit(solution)/shard_map/mn,nlk->mlk/dot_general | solution.py:44
  35.7 3.1 %collective-permute-start.8 = (f32[128,8,128]{0,2,1:T(8,128)S(1)}, f32[128,8,128]{0,2,1:T(8,128)S(1)}, u32[]{:S(2)}, u32[]{:S(2)}) collective-permute-start(f32[128,8,128]{0,2,1:T(8,128)S(1)} %fusion.3), channel_id=1, source_target_pairs={{0,16},{1,17},{2,18},{3,19},{4,20},{5,21},{6,22},{7,23},{8,24},{9,... | collective-permute-start | bytes 1572872 | tf_op jit(solution)/shard_map/ppermute | solution.py:29
  38.9 11.0 %collective-permute-done.8 = f32[128,8,128]{0,2,1:T(8,128)S(1)} collective-permute-done((f32[128,8,128]{0,2,1:T(8,128)S(1)}, f32[128,8,128]{0,2,1:T(8,128)S(1)}, u32[]{:S(2)}, u32[]{:S(2)}) %collective-permute-start.8) | collective-permute-done | bytes 524320 | tf_op jit(solution)/shard_map/ppermute | solution.py:29
  50.0 1.0 %gather_fusion = f32[512,128]{1,0:T(8,128)S(1)} fusion(f32[128,1024]{0,1:T(8,128)S(1)} %bitcast.85, s32[1024]{0:T(1024)S(1)} %pad_clamp_fusion.3), kind=kCustom, calls=%fused_computation.clone | custom fusion | bytes 526336 | tf_op jit(solution)/shard_map/jit(_take)/gather | solution.py:72
  51.0 1.0 %gather_fusion.1 = f32[512,128]{1,0:T(8,128)S(1)} fusion(f32[128,1024]{0,1:T(8,128)S(1)} %bitcast.86, s32[1024]{0:T(1024)S(1)} %pad_clamp_fusion.2), kind=kCustom, calls=%fused_computation.1.clone | custom fusion | bytes 526336 | tf_op jit(solution)/shard_map/jit(_take)/gather | solution.py:74
  52.1 1.0 %gather_fusion.2 = f32[512,128]{1,0:T(8,128)S(1)} fusion(f32[128,1024]{0,1:T(8,128)S(1)} %bitcast.87, s32[1024]{0:T(1024)S(1)} %pad_clamp_fusion.1), kind=kCustom, calls=%fused_computation.2.clone | custom fusion | bytes 526336 | tf_op jit(solution)/shard_map/jit(_take)/gather | solution.py:74
  53.1 1.0 %gather_fusion.3 = f32[512,128]{1,0:T(8,128)S(1)} fusion(f32[128,1024]{0,1:T(8,128)S(1)} %bitcast.88, s32[1024]{0:T(1024)S(1)} %pad_clamp_fusion), kind=kCustom, calls=%fused_computation.3.clone | custom fusion | bytes 526336 | tf_op jit(solution)/shard_map/jit(_take)/gather | solution.py:74
  54.9 0.8 %broadcast_multiply_fusion = f32[128,4,128]{0,2,1:T(8,128)} fusion(f32[128,4,128]{0,2,1:T(8,128)S(1)} %bitcast.93, f32[4,128]{1,0:T(4,128)S(1)} %fusion.101), kind=kLoop, calls=%fused_computation.108 | loop fusion | flops 65536 | bytes 526336 | tf_op jit(solution)/shard_map/mul | solution.py:80
  55.8 3.4 %all-to-all-start = ((f32[128,4,128]{0,2,1:T(8,128)}), f32[128,4,128]{0,2,1:T(8,128)S(1)}, u32[]{:S(2)}, u32[]{:S(2)}) async-start(f32[128,4,128]{0,2,1:T(8,128)} %broadcast_multiply_fusion), calls=%async_computation | async-start | bytes 524288 | tf_op jit(solution)/shard_map/all_to_all | solution.py:85
  59.2 1.0 %copy.10 = f32[1,128,8,128]{3,2,1,0:T(8,128)} copy(f32[1,128,8,128]{1,3,2,0:T(8,128)S(1)} %bitcast.89) | data formatting | bytes 1048576
  60.2 3.7 %all-to-all-done = f32[128,4,128]{0,2,1:T(8,128)S(1)} async-done(((f32[128,4,128]{0,2,1:T(8,128)}), f32[128,4,128]{0,2,1:T(8,128)S(1)}, u32[]{:S(2)}, u32[]{:S(2)}) %all-to-all-start) | async-done | bytes 262176 | tf_op jit(solution)/shard_map/all_to_all | solution.py:85
  64.3 0.8 %copy.11 = f32[1,128,512]{2,1,0:T(8,128)} copy(f32[1,128,512]{1,2,0:T(8,128)S(1)} %bitcast.94) | data formatting | bytes 524288
  (47 shorter events, 3.1 us)
Async XLA Ops:
  0.6 26.9 %copy-start = (f32[128,128]{1,0:T(8,128)S(1)}, f32[128,128]{1,0:T(8,128)}, u32[]{:S(2)}) copy-start(f32[128,128]{1,0:T(8,128)} %param.11) | copy-start | bytes 196612
  0.6 5.6 %copy-start.1 = (f32[2,1,8,128]{3,2,1,0:T(8,128)S(1)}, f32[2,1,8,128]{3,2,1,0:T(8,128)}, u32[]{:S(2)}) copy-start(f32[2,1,8,128]{3,2,1,0:T(8,128)} %param.10) | copy-start | bytes 24580
  0.7 8.9 %copy-start.3 = (s32[4,1,512]{2,1,0:T(1,128)S(1)}, s32[4,1,512]{2,1,0:T(1,128)}, u32[]{:S(2)}) copy-start(s32[4,1,512]{2,1,0:T(1,128)} %param.12) | copy-start | bytes 24580
  0.7 9.0 %copy-start.5 = (s32[1,1,4]{2,1,0:T(1,128)S(1)}, s32[1,1,4]{2,1,0:T(1,128)}, u32[]{:S(2)}) copy-start(s32[1,1,4]{2,1,0:T(1,128)} %param.14) | copy-start | bytes 52
  2.0 21.9 %collective-permute-start = (f32[128,4,128]{0,2,1:T(8,128)S(1)}, f32[128,4,128]{0,2,1:T(8,128)S(1)}, u32[]{:S(2)}, u32[]{:S(2)}) collective-permute-start(f32[128,4,128]{0,2,1:T(8,128)S(1)} %get-tuple-element.7), channel_id=1, source_target_pairs={{0,4},{4,8},{8,12},{12,0},{1,5},{5,9},{9,13},{13,1},{2,6},{6,10},{... | collective-permute-start | bytes 786440 | tf_op jit(solution)/shard_map/ppermute | solution.py:18
  4.2 19.7 %collective-permute-start.1 = (f32[128,4,128]{0,2,1:T(8,128)S(1)}, f32[128,4,128]{0,2,1:T(8,128)S(1)}, u32[]{:S(2)}, u32[]{:S(2)}) collective-permute-start(f32[128,4,128]{0,2,1:T(8,128)S(1)} %get-tuple-element.8), channel_id=1, source_target_pairs={{4,0},{8,4},{12,8},{0,12},{5,1},{9,5},{13,9},{1,13},{6,2},{10,6},{... | collective-permute-start | bytes 786440 | tf_op jit(solution)/shard_map/ppermute | solution.py:21
  6.3 11.4 %collective-permute-start.4 = (f32[2,4,128]{2,1,0:T(4,128)S(1)}, f32[2,4,128]{2,1,0:T(4,128)S(1)}, u32[]{:S(2)}, u32[]{:S(2)}) collective-permute-start(f32[2,4,128]{2,1,0:T(4,128)S(1)} %get-tuple-element.27), channel_id=1, source_target_pairs={{0,4},{4,8},{8,12},{12,0},{1,5},{5,9},{9,13},{13,1},{2,6},{6,10},{... | collective-permute-start | bytes 12296 | tf_op jit(solution)/shard_map/ppermute | solution.py:18
  6.3 11.4 %collective-permute-start.5 = (f32[2,4,128]{2,1,0:T(4,128)S(1)}, f32[2,4,128]{2,1,0:T(4,128)S(1)}, u32[]{:S(2)}, u32[]{:S(2)}) collective-permute-start(f32[2,4,128]{2,1,0:T(4,128)S(1)} %get-tuple-element.28), channel_id=1, source_target_pairs={{4,0},{8,4},{12,8},{0,12},{5,1},{9,5},{13,9},{1,13},{6,2},{10,6},{... | collective-permute-start | bytes 12296 | tf_op jit(solution)/shard_map/ppermute | solution.py:21
  17.8 3.6 %collective-permute-start.6 = (f32[2,16,4]{2,1,0:T(8,128)S(1)}, f32[2,16,4]{2,1,0:T(8,128)S(1)}, u32[]{:S(2)}, u32[]{:S(2)}) collective-permute-start(f32[2,16,4]{2,1,0:T(8,128)S(1)} %get-tuple-element.15), channel_id=1, source_target_pairs={{0,1},{1,2},{2,3},{3,0},{4,5},{5,6},{6,7},{7,4},{8,9},{9,10},{10,1... | collective-permute-start | bytes 1544 | tf_op jit(solution)/shard_map/ppermute | solution.py:18
  20.5 3.2 %collective-permute-start.7 = (f32[2,16,4]{2,1,0:T(8,128)S(1)}, f32[2,16,4]{2,1,0:T(8,128)S(1)}, u32[]{:S(2)}, u32[]{:S(2)}) collective-permute-start(f32[2,16,4]{2,1,0:T(8,128)S(1)} %get-tuple-element.16), channel_id=1, source_target_pairs={{1,0},{2,1},{3,2},{0,3},{5,4},{6,5},{7,6},{4,7},{9,8},{10,9},{11,1... | collective-permute-start | bytes 1544 | tf_op jit(solution)/shard_map/ppermute | solution.py:21
  23.9 1.3 %collective-permute-start.2 = (f32[128,16,4]{0,2,1:T(4,128)S(1)}, f32[128,16,4]{0,2,1:T(4,128)S(1)}, u32[]{:S(2)}, u32[]{:S(2)}) collective-permute-start(f32[128,16,4]{0,2,1:T(4,128)S(1)} %get-tuple-element.5), channel_id=1, source_target_pairs={{0,1},{1,2},{2,3},{3,0},{4,5},{5,6},{6,7},{7,4},{8,9},{9,10},{10,1... | collective-permute-start | bytes 98312 | tf_op jit(solution)/shard_map/ppermute | solution.py:18
  24.0 3.4 %collective-permute-start.3 = (f32[128,16,4]{0,2,1:T(4,128)S(1)}, f32[128,16,4]{0,2,1:T(4,128)S(1)}, u32[]{:S(2)}, u32[]{:S(2)}) collective-permute-start(f32[128,16,4]{0,2,1:T(4,128)S(1)} %get-tuple-element.6), channel_id=1, source_target_pairs={{1,0},{2,1},{3,2},{0,3},{5,4},{6,5},{7,6},{4,7},{9,8},{10,9},{11,1... | collective-permute-start | bytes 98312 | tf_op jit(solution)/shard_map/ppermute | solution.py:21
  34.2 4.7 %copy-start.4 = (f32[4,1,512]{2,1,0:T(1,128)S(1)}, f32[4,1,512]{2,1,0:T(1,128)}, u32[]{:S(2)}) copy-start(f32[4,1,512]{2,1,0:T(1,128)} %param.13) | copy-start | bytes 24580
  35.7 14.2 %collective-permute-start.8 = (f32[128,8,128]{0,2,1:T(8,128)S(1)}, f32[128,8,128]{0,2,1:T(8,128)S(1)}, u32[]{:S(2)}, u32[]{:S(2)}) collective-permute-start(f32[128,8,128]{0,2,1:T(8,128)S(1)} %fusion.3), channel_id=1, source_target_pairs={{0,16},{1,17},{2,18},{3,19},{4,20},{5,21},{6,22},{7,23},{8,24},{9,... | collective-permute-start | bytes 1572872 | tf_op jit(solution)/shard_map/ppermute | solution.py:29
  54.9 9.0 %copy-start.2 = (f32[1,1,128,128]{3,2,1,0:T(8,128)S(1)}, f32[1,1,128,128]{3,2,1,0:T(8,128)}, u32[]{:S(2)}) copy-start(f32[1,1,128,128]{3,2,1,0:T(8,128)} %param.15) | copy-start | bytes 196612
  55.8 8.1 %all-to-all-start = ((f32[128,4,128]{0,2,1:T(8,128)}), f32[128,4,128]{0,2,1:T(8,128)S(1)}, u32[]{:S(2)}, u32[]{:S(2)}) async-start(f32[128,4,128]{0,2,1:T(8,128)} %broadcast_multiply_fusion), calls=%async_computation | async-start | bytes 524288 | tf_op jit(solution)/shard_map/all_to_all | solution.py:85
where the time goes:
time: 66.3 us; the launch traced here: 65.2 us
  waiting for transfers between devices  28.7 us (43%)
  starting transfers between devices  17.3 us (26%)
  matrix products  8.55 us (13%)
  local copies, waits for them, and re-layouts  7.66 us (12%)
  other arithmetic  2.01 us (3%)
  between operations  0.93 us (1%)
    ppermute x1, waiting for transfers between devices, passed_along(): return lax.ppermute(x, axis, pairs)  11 us
    ppermute x4, waiting for transfers between devices, padded_2(): lax.ppermute(lax.slice_in_dim(block, block.shape[dim] - width, None, axis...  9.44 us
    dot_general x4, matrix products, advance_slot(): jnp.einsum('mn,nlk->mlk', mixing, shifted_state, precision=lax.Precision....  8.17 us
    ppermute x4, starting transfers between devices, padded_2(): lax.ppermute(lax.slice_in_dim(block, 0, width, axis=dim), axis, backward)  5.83 us
    ppermute x4, starting transfers between devices, padded_2(): lax.ppermute(lax.slice_in_dim(block, block.shape[dim] - width, None, axis...  4.96 us
    ppermute x4, waiting for transfers between devices, padded_2(): lax.ppermute(lax.slice_in_dim(block, 0, width, axis=dim), axis, backward)  4.5 us
    all_to_all x1, waiting for transfers between devices, local(): lax.all_to_all(profile, 'obs', split_axis=1, concat_axis=1, tiled=True)  3.74 us
    all_to_all x1, starting transfers between devices, local(): lax.all_to_all(profile, 'obs', split_axis=1, concat_axis=1, tiled=True)  3.4 us
  transfers between devices with their start and end apart: 10, of which 7 were waited for; matrix products, arithmetic and copies ran while one was open for 2% of the time, Pallas kernels for 0%

commit v1 on v0

v1 whole, which is shorter than its diff:
```python
import functools

import jax
import jax.numpy as jnp
from jax import lax
from jax.experimental import pallas as pl
from jax.experimental.pallas import tpu as pltpu
from jax.sharding import PartitionSpec as P

STEPS = 4
mixing_rate = 0.15
MESH = pl.DeviceIdType.MESH
SUB = 8
LANES = 128

TILE_DIRS = ((1, 0), (-1, 0))
EDGE_DIRS = ((0, 1), (0, -1), (1, 1), (1, -1), (-1, 1), (-1, -1))
DIRS = TILE_DIRS + EDGE_DIRS


def halves(x):
    high = x.astype(jnp.bfloat16)
    return high, (x - high.astype(jnp.float32)).astype(jnp.bfloat16)


def dot(a, b):
    return jnp.dot(a, b, preferred_element_type=jnp.float32)


def dot3(a, b):
    return dot(a[0], b[0]) + (dot(a[0], b[1]) + dot(a[1], b[0]))


def exact(a, b):
    return jnp.dot(a, b, precision=lax.Precision.HIGHEST, preferred_element_type=jnp.float32)


def kernel(
    n_slot, n_tile, n_obs,
    f_ref, winds_ref, mixing_ref, cells_ref, weights_ref, counts_ref, jac_ref,
    state_ref, rad_ref,
    ft, halo, packed, edges, rates, coef, gs, gr, w_hi, w_lo, pf, rf, pg, rg,
    halo_send, halo_recv, edge_send, edge_recv, rate_send, rate_recv,
    g_send, g_recv, pf_send, pf_recv, pg_send, pg_recv,
):
    slot = lax.axis_index("slot")
    tile = lax.axis_index("tile")
    obs = lax.axis_index("obs")
    cx, levels, cy = ft.shape
    rows = cells_ref.shape[1]
    cap = rows // n_obs
    span = cx * 2 * STEPS
    groups = LANES // span
    depth = SUB * groups
    chunks = levels // depth

    def neighbour(dt, do):
        return {"slot": slot, "tile": lax.rem(tile + dt + n_tile, n_tile), "obs": lax.rem(obs + do + n_obs, n_obs)}

    def peer(by):
        return {"slot": slot, "tile": tile, "obs": lax.rem(obs + by, n_obs)}

    def along(by):
        return {"slot": lax.rem(slot + by + n_slot, n_slot), "tile": tile, "obs": obs}

    def remote(src, dst, send, recv, to):
        return pltpu.make_async_remote_copy(
            src_ref=src, dst_ref=dst, send_sem=send, recv_sem=recv, device_id=to, device_id_type=MESH
        )

    def part(c):
        return pl.ds(pl.multiple_of(c * depth, depth), depth)

    def halo_copy(k, c):
        first = cx - STEPS if k == 0 else 0
        return remote(
            ft.at[pl.ds(first, STEPS), part(c), :], halo.at[k, :, part(c), :],
            halo_send.at[k, c], halo_recv.at[k, c], neighbour(*TILE_DIRS[k]),
        )

    def edge_copy(k, c):
        return remote(
            packed.at[c], edges.at[k, c], edge_send.at[k, c], edge_recv.at[k, c], neighbour(*EDGE_DIRS[k])
        )

    def rate_copy(k):
        return remote(winds_ref, rates.at[k], rate_send.at[k], rate_recv.at[k], neighbour(*DIRS[k]))

    def g_copy(c):
        return remote(
            gs.at[:, part(c), :], gr.at[:, part(c), :], g_send.at[c], g_recv.at[c], along(1)
        )

    def pf_copy(by):
        return remote(
            pf.at[lax.rem(obs + by, n_obs)], rf.at[obs], pf_send.at[by], pf_recv.at[by], peer(by)
        )

    def pg_copy(by, c):
        return remote(
            pg.at[lax.rem(obs + by, n_obs), part(c), :], rg.at[obs, part(c), :],
            pg_send.at[by, c], pg_recv.at[by, c], peer(by),
        )

    def each_chunk(body):
        def step(c, carry):
            body(c)
            return carry

        lax.fori_loop(0, chunks, step, 0)

    lane = lax.broadcasted_iota(jnp.int32, (SUB, LANES), 1)

    def pack(src):
        def one(c):
            out = jnp.zeros((SUB, LANES), jnp.float32)
            for h in range(groups):
                for x in range(cx):
                    level = pl.multiple_of(c * depth + h * SUB, SUB)
                    v = src[pl.ds(level * cx + x, SUB, stride=cx), :]
                    ft[x, pl.ds(level, SUB), :] = v
                    low = h * span + x * 2 * STEPS
                    moved = pltpu.roll(v, (low + STEPS) % LANES, 1)
                    out = jnp.where((lane >= low) & (lane < low + 2 * STEPS), moved, out)
            packed[c] = out

        each_chunk(one)

    def send_halos():
        def one(c):
            for k in range(len(TILE_DIRS)):
                halo_copy(k, c).start()
            for k in range(len(EDGE_DIRS)):
                edge_copy(k, c).start()

        each_chunk(one)

    def source_of(x):
        if x < 0:
            return 1, x + cx
        if x >= cx:
            return -1, x - cx
        return 0, x

    def forward():
        for k in range(len(DIRS)):
            rate_copy(k).wait_recv()
        for x in range(1 - STEPS, cx + STEPS - 1):
            dt, row = source_of(x)
            for which in range(2):
                def spread(ref):
                    return jnp.broadcast_to(ref[which, pl.ds(row, 1), :], (SUB, LANES))

                main = spread(winds_ref) if dt == 0 else spread(rates.at[DIRS.index((dt, 0))])
                west = spread(rates.at[DIRS.index((dt, 1))])
                east = spread(rates.at[DIRS.index((dt, -1))])
                side = jnp.where(lane < LANES // 2, east, west)
                for place, rate in ((0, main), (1, side)):
                    coef[x + STEPS, place, 2 * which] = mixing_rate + rate
                    coef[x + STEPS, place, 2 * which + 1] = mixing_rate - rate

        first_lane = lane == 0
        last_lane = lane == LANES - 1
        lower = lax.rem(lane, 2 * STEPS) < STEPS

        def one(c):
            for k in range(len(TILE_DIRS)):
                halo_copy(k, c).wait_recv()
            for k in range(len(EDGE_DIRS)):
                edge_copy(k, c).wait_recv()

            def group(h, carry):
                level = pl.ds(pl.multiple_of(c * depth + h * SUB, SUB), SUB)
                joined = {
                    dt: jnp.where(lower, edges[EDGE_DIRS.index((dt, 1)), c], edges[EDGE_DIRS.index((dt, -1)), c])
                    for dt in (-1, 0, 1)
                }
                joined = {dt: pltpu.roll(v, LANES - h * span, 1) for dt, v in joined.items()}
                main, side = {}, {}
                for x in range(-STEPS, cx + STEPS):
                    dt, row = source_of(x)
                    if dt == 0:
                        main[x] = ft[row, level, :]
                    elif dt == 1:
                        main[x] = halo[0, row - (cx - STEPS), level, :]
                    else:
                        main[x] = halo[1, row, level, :]
                    side[x] = pltpu.roll(joined[dt], (-(row * 2 * STEPS + STEPS)) % LANES, 1)
                for step in range(STEPS):
                    new_main, new_side = {}, {}
                    for x in range(step + 1 - STEPS, cx + STEPS - 1 - step):
                        m, e = main[x], side[x]
                        m_up, e_up = pltpu.roll(m, 1, 1), pltpu.roll(e, 1, 1)
                        m_down, e_down = pltpu.roll(m, LANES - 1, 1), pltpu.roll(e, LANES - 1, 1)

                        def mixed(place, centre, east, west, north, south):
                            k = x + STEPS
                            return (
                                (1.0 - 4.0 * mixing_rate) * centre
                                + (coef[k, place, 0] * east + coef[k, place, 1] * west)
                                + (coef[k, place, 2] * north + coef[k, place, 3] * south)
                            )

                        new_main[x] = mixed(
                            0, m, main[x + 1], main[x - 1],
                            jnp.where(last_lane, e_down, m_down), jnp.where(first_lane, e_up, m_up),
                        )
                        if step < STEPS - 1:
                            new_side[x] = mixed(
                                1, e, side[x + 1], side[x - 1],
                                jnp.where(last_lane, m_down, e_down), jnp.where(first_lane, m_up, e_up),
                            )
                    main, side = new_main, new_side
                for x in range(cx):
                    gs[x, level, :] = main[x]
                return carry

            lax.fori_loop(0, groups, group, 0)
            g_copy(c).start()

        each_chunk(one)

    barrier = pltpu.get_barrier_semaphore()
    greeted = [neighbour(*d) for d in DIRS] + [peer(by) for by in range(1, n_obs)] + [along(1), along(-1)]
    for to in greeted:
        pl.semaphore_signal(barrier, inc=1, device_id=to, device_id_type=MESH)

    @pl.when(slot == 0)
    def _():
        pack(f_ref)

    pl.semaphore_wait(barrier, len(greeted))

    @pl.when(slot < n_slot - 1)
    def _():
        for k in range(len(DIRS)):
            rate_copy(k).start()

    @pl.when(slot == 0)
    def _():
        send_halos()
        forward()

    tall = cy
    base = lax.broadcasted_iota(jnp.int32, (tall, cap), 0)
    live_row = lax.broadcasted_iota(jnp.int32, (1, cap), 1)

    def owner_weights(q, carry):
        cols = pl.ds(pl.multiple_of(q * cap, cap), cap)
        live = live_row < counts_ref[0, q]
        cell = [cells_ref[pl.ds(p, 1), cols] for p in range(cells_ref.shape[0])]
        weight = [jnp.where(live, weights_ref[pl.ds(p, 1), cols], 0.0) for p in range(cells_ref.shape[0])]

        def row_weights(x, inner):
            total = jnp.zeros((tall, cap), jnp.float32)
            for p in range(len(cell)):
                total = total + jnp.where(base == cell[p] - x * tall, weight[p], 0.0)
            high, low = halves(total)
            at = pl.ds(pl.multiple_of(x * tall, tall), tall)
            w_hi[at, cols] = high
            w_lo[at, cols] = low
            return inner

        lax.fori_loop(0, cx, row_weights, 0)
        return carry

    lax.fori_loop(0, n_obs, owner_weights, 0)

    wide = 2 * cap if n_obs % 2 == 0 else cap

    def interpolate(pieces, keep):
        parts = [halves(v) for v in pieces]
        high = jnp.concatenate([p[0] for p in parts], axis=1)
        low = jnp.concatenate([p[1] for p in parts], axis=1)
        both = jnp.concatenate([high, low], axis=0)
        tall_in = high.shape[0]

        def one(b, carry):
            cols = pl.ds(pl.multiple_of(b * wide, wide), wide)
            main = dot(both, w_hi[:, cols])
            total = main[:tall_in] + (main[tall_in:] + dot(high, w_lo[:, cols]))
            for j in range(wide // cap):
                keep(b * (wide // cap) + j, total[:, j * cap : (j + 1) * cap])
            return carry

        lax.fori_loop(0, rows // wide, one, 0)

    def keep_pf(q, value):
        pf[q] = value

    interpolate([f_ref[pl.ds(x, levels, stride=cx), :] for x in range(cx)], keep_pf)
    for by in range(1, n_obs):
        pf_copy(by).start()

    eye = jnp.where(
        lax.broadcasted_iota(jnp.int32, (levels, levels), 0) == lax.broadcasted_iota(jnp.int32, (levels, levels), 1),
        1.0, 0.0,
    )
    power = eye + mixing_ref[...]
    for _ in range(STEPS.bit_length() - 1):
        power = exact(power, power)
    jac = jac_ref[...]

    @pl.when(slot > 0)
    def _():
        def one(c):
            g_copy(c).wait_recv()

            def keep_pg(q, value):
                pg[q, part(c), :] = value

            interpolate([gr[x, part(c), :] for x in range(cx)], keep_pg)
            for by in range(1, n_obs):
                pg_copy(by, c).start()

        each_chunk(one)
        power_parts = halves(power)

        for x in range(cx):
            state = dot3(power_parts, halves(gr[x])) + f_ref[pl.ds(x, levels, stride=cx), :]
            state_ref[pl.ds(x, levels, stride=cx), :] = state

    @pl.when(slot == 0)
    def _():
        state_ref[...] = f_ref[...]

    if n_slot > 2:
        @pl.when((slot > 0) & (slot < n_slot - 1))
        def _():
            pack(state_ref)
            send_halos()
            forward()

    def owner_out(o, value):
        rad_ref[:, pl.ds(pl.multiple_of(o * cap, cap), cap)] = value

    rf[obs] = pf[obs]
    for by in range(1, n_obs):
        pf_copy(by).wait_recv()

    @pl.when(slot > 0)
    def _():
        rg[obs] = pg[obs]

        def arrived(c):
            for by in range(1, n_obs):
                pg_copy(by, c).wait_recv()

        each_chunk(arrived)
        table = halves(jnp.concatenate([jac, exact(jac, power)], axis=1))

        def one(o, carry):
            owner_out(o, dot3(table, halves(jnp.concatenate([rf[o], rg[o]], axis=0))))
            return carry

        lax.fori_loop(0, n_obs, one, 0)

    @pl.when(slot == 0)
    def _():
        table = halves(jac)

        def one(o, carry):
            owner_out(o, dot3(table, halves(rf[o])))
            return carry

        lax.fori_loop(0, n_obs, one, 0)

    for by in range(1, n_obs):
        pf_copy(by).wait_send()

    @pl.when(slot > 0)
    def _():
        def left(c):
            for by in range(1, n_obs):
                pg_copy(by, c).wait_send()

        each_chunk(left)

    @pl.when(slot < n_slot - 1)
    def _():
        for k in range(len(DIRS)):
            rate_copy(k).wait_send()

        def left(c):
            for k in range(len(TILE_DIRS)):
                halo_copy(k, c).wait_send()
            for k in range(len(EDGE_DIRS)):
                edge_copy(k, c).wait_send()
            g_copy(c).wait_send()

        each_chunk(left)


def solution(mesh):
    n_slot, n_tile, n_obs = (mesh.shape[a] for a in ("slot", "tile", "obs"))

    def local(forcing, winds, mixing, observation_columns, obs_weights, obs_counts, jacobian):
        _, levels, cx, cy = forcing.shape
        rows = observation_columns.shape[2]
        cap = rows // n_obs
        channels = jacobian.shape[2]
        chunks = levels // (SUB * (LANES // (cx * 2 * STEPS)))
        f32, bf16 = jnp.float32, jnp.bfloat16
        dma = pltpu.SemaphoreType.DMA
        vmem = pl.BlockSpec(memory_space=pltpu.VMEM)
        states, radiances = pl.pallas_call(
            functools.partial(kernel, n_slot, n_tile, n_obs),
            out_shape=(
                jax.ShapeDtypeStruct((levels * cx, cy), f32),
                jax.ShapeDtypeStruct((channels, rows), f32),
            ),
            in_specs=[vmem] * 5 + [pl.BlockSpec(memory_space=pltpu.SMEM), vmem],
            out_specs=(vmem, vmem),
            scratch_shapes=[
                pltpu.VMEM((cx, levels, cy), f32),
                pltpu.VMEM((2, STEPS, levels, cy), f32),
                pltpu.VMEM((chunks, SUB, LANES), f32),
                pltpu.VMEM((len(EDGE_DIRS), chunks, SUB, LANES), f32),
                pltpu.VMEM((len(DIRS), 2, cx, cy), f32),
                pltpu.VMEM((cx + 2 * STEPS, 2, 4, SUB, LANES), f32),
                pltpu.VMEM((cx, levels, cy), f32),
                pltpu.VMEM((cx, levels, cy), f32),
                pltpu.VMEM((cx * cy, rows), bf16),
                pltpu.VMEM((cx * cy, rows), bf16),
                pltpu.VMEM((n_obs, levels, cap), f32),
                pltpu.VMEM((n_obs, levels, cap), f32),
                pltpu.VMEM((n_obs, levels, cap), f32),
                pltpu.VMEM((n_obs, levels, cap), f32),
                dma((2, chunks)), dma((2, chunks)),
                dma((len(EDGE_DIRS), chunks)), dma((len(EDGE_DIRS), chunks)),
                dma((len(DIRS),)), dma((len(DIRS),)),
                dma((chunks,)), dma((chunks,)),
                dma((n_obs,)), dma((n_obs,)),
                dma((n_obs, chunks)), dma((n_obs, chunks)),
            ],
            compiler_params=pltpu.CompilerParams(
                collective_id=0, has_side_effects=True, vmem_limit_bytes=48 * 1024 * 1024
            ),
        )(
            forcing.reshape(levels * cx, cy),
            winds.reshape(2, cx, cy),
            mixing,
            observation_columns.reshape(-1, rows),
            obs_weights.reshape(-1, rows),
            obs_counts.reshape(1, n_obs),
            jacobian.reshape(channels, levels),
        )
        return states.reshape(1, levels, cx, cy), radiances.reshape(1, channels, rows)

    return jax.shard_map(
        local,
        mesh=mesh,
        in_specs=(
            P("slot", None, "tile", "obs"),
            P(None, "slot", "tile", "obs"),
            P(),
            P(None, "slot", ("tile", "obs")),
            P(None, "slot", ("tile", "obs")),
            P("slot", ("tile", "obs"), None),
            P("slot", "obs", None, None),
        ),
        out_specs=(P("slot", None, "tile", "obs"), P("slot", None, ("tile", "obs"))),
        check_vma=False,
    )
```

time: 66.3 us -> 40.1 us (0.60); the launches traced: 65.2 us -> 39.8 us
  Pallas kernels: 0 us -> 33.5 us
  waiting for transfers between devices: 28.7 us -> 0 us
  starting transfers between devices: 17.3 us -> 0 us
  matrix products: 8.55 us -> 0 us
  local copies, waits for them, and re-layouts: 7.66 us -> 5.62 us
  other arithmetic: 2.01 us -> 0 us
    pallas_call x0 -> x1, Pallas kernels: none -> 33.5 us  [local(): pl.pallas_call(functools.partial(kernel, n_slot, n_tile, n_obs), out_shap...]
    ppermute x9 -> x0, waiting for transfers between devices: 24.9 us -> none  [the longest x1 11 us: passed_along(): return lax.ppermute(x, axis, pairs)]
    ppermute x9 -> x0, starting transfers between devices: 13.9 us -> none  [the longest x4 5.83 us: padded_2(): lax.ppermute(lax.slice_in_dim(block, 0, width, axis=dim), axis, backward)]
    dot_general x5 -> x0, matrix products: 8.55 us -> none  [the longest x4 8.17 us: advance_slot(): jnp.einsum('mn,nlk->mlk', mixing, shifted_state, precision=lax.Precision....]
    gather x4 -> x0, local copies, waits for them, and re-layouts: 4.15 us -> none  [the longest x3 3.11 us: local(): profile = profile + weights[corner] * jnp.take(flat, cells[corner], axis=1)]
    all_to_all x1 -> x0, waiting for transfers between devices: 3.74 us -> none  [local(): lax.all_to_all(profile, 'obs', split_axis=1, concat_axis=1, tiled=True)]
    all_to_all x1 -> x0, starting transfers between devices: 3.4 us -> none  [local(): lax.all_to_all(profile, 'obs', split_axis=1, concat_axis=1, tiled=True)]
    unnamed x15 -> x16, local copies, waits for them, and re-layouts: 3.15 us -> 5.62 us
  transfers between devices with their start and end apart: 10 -> 0, of which waited for: 7 -> 0; matrix products, arithmetic and copies ran while one was open for 2% -> 0% of each run, Pallas kernels for 0% -> 0%
where the time goes in v1:
time: 40.1 us; the launch traced here: 39.8 us
  Pallas kernels  33.5 us (84%)
  local copies, waits for them, and re-layouts  5.62 us (14%)
  between operations  0.66 us (2%)
    pallas_call x1, Pallas kernels, local(): pl.pallas_call(functools.partial(kernel, n_slot, n_tile, n_obs), out_shap...  33.5 us
    unnamed x16, local copies, waits for them, and re-layouts  5.62 us

profile of v1, /device:TPU:1, one launch (start us, length us, event | category | flops | bytes accessed | tf_op | source)
XLA Modules:
  0.0 39.8 jit_solution(3836500665621112847)
XLA Ops:
  0.6 0.0 copy-start.5
  0.6 0.7 %copy.14 = s32[4,1,512]{2,0,1:T(4,128)S(1)} copy(s32[4,1,512]{2,1,0:T(1,128)} %param.10) | data formatting | bytes 16384
  1.3 0.0 copy-done.5
  1.3 0.0 copy-start.3
  1.4 0.0 copy-start.4
  1.4 0.7 %copy-done.3 = f32[2,1,8,128]{3,2,1,0:T(8,128)S(1)} copy-done((f32[2,1,8,128]{3,2,1,0:T(8,128)S(1)}, f32[2,1,8,128]{3,2,1,0:T(8,128)}, u32[]{:S(2)}) %copy-start.3) | copy-done | bytes 8216
  2.0 0.0 copy-done.4
  2.0 0.0 copy-start
  2.1 1.0 %copy-done = f32[1,128,8,128]{3,2,1,0:T(8,128)S(1)} copy-done((f32[1,128,8,128]{3,2,1,0:T(8,128)S(1)}, f32[1,128,8,128]{3,2,1,0:T(8,128)}, u32[]{:S(2)}) %copy-start) | copy-done | bytes 524312
  3.1 0.0 copy-start.1
  3.1 0.8 %copy-done.1 = f32[128,128]{1,0:T(8,128)S(1)} copy-done((f32[128,128]{1,0:T(8,128)S(1)}, f32[128,128]{1,0:T(8,128)}, u32[]{:S(2)}) %copy-start.1) | copy-done | bytes 65560
  3.9 0.0 copy-start.2
  3.9 0.8 %copy-done.2 = f32[1,1,128,128]{3,2,1,0:T(8,128)S(1)} copy-done((f32[1,1,128,128]{3,2,1,0:T(8,128)S(1)}, f32[1,1,128,128]{3,2,1,0:T(8,128)}, u32[]{:S(2)}) %copy-start.2) | copy-done | bytes 65560
  4.8 33.5 %shard_map.86 = (f32[1024,128]{1,0:T(8,128)S(1)}, f32[128,512]{1,0:T(8,128)S(1)}) custom-call(f32[1024,128]{1,0:T(8,128)S(1)} %bitcast.12, f32[2,8,128]{2,1,0:T(8,128)S(1)} %bitcast.18, f32[128,128]{1,0:T(8,128)S(1)} %copy-done.1, s32[4,512]{1,0:T(4,128)S(1)} %bitcast.16, f32[4,512]{1,0:T(4,128)S(1)} %bitcast.17, s32[1,4]{1,0:T(1,128)S(1)} %bitcast.19, ...), custom_call_target="tpu_custom_call" | custom-call | tf_op jit(solution)/shard_map/pallas_call | solution.py:406
  38.3 0.8 %copy.17 = f32[1,128,8,128]{3,2,1,0:T(8,128)} copy(f32[1,128,8,128]{3,2,1,0:T(8,128)S(1)} %bitcast.13) | data formatting | bytes 1048576
  39.1 0.7 %copy.18 = f32[1,128,512]{2,1,0:T(8,128)} copy(f32[1,128,512]{2,1,0:T(8,128)S(1)} %bitcast.14) | data formatting | bytes 524288
  (1 shorter events, 0.0 us)
Async XLA Ops:
  0.6 0.7 %copy-start.5 = (f32[4,1,512]{2,1,0:T(1,128)S(1)}, f32[4,1,512]{2,1,0:T(1,128)}, u32[]{:S(2)}) copy-start(f32[4,1,512]{2,1,0:T(1,128)} %param.11) | copy-start | bytes 24580
  1.3 0.7 %copy-start.3 = (f32[2,1,8,128]{3,2,1,0:T(8,128)S(1)}, f32[2,1,8,128]{3,2,1,0:T(8,128)}, u32[]{:S(2)}) copy-start(f32[2,1,8,128]{3,2,1,0:T(8,128)} %param.8) | copy-start | bytes 24580
  1.4 0.7 %copy-start.4 = (s32[1,1,4]{2,1,0:T(1,128)S(1)}, s32[1,1,4]{2,1,0:T(1,128)}, u32[]{:S(2)}) copy-start(s32[1,1,4]{2,1,0:T(1,128)} %param.12) | copy-start | bytes 52
  2.0 1.0 %copy-start = (f32[1,128,8,128]{3,2,1,0:T(8,128)S(1)}, f32[1,128,8,128]{3,2,1,0:T(8,128)}, u32[]{:S(2)}) copy-start(f32[1,128,8,128]{3,2,1,0:T(8,128)} %param.7) | copy-start | bytes 1572868
  3.1 0.8 %copy-start.1 = (f32[128,128]{1,0:T(8,128)S(1)}, f32[128,128]{1,0:T(8,128)}, u32[]{:S(2)}) copy-start(f32[128,128]{1,0:T(8,128)} %mixing_ref.1) | copy-start | bytes 196612
  3.9 0.8 %copy-start.2 = (f32[1,1,128,128]{3,2,1,0:T(8,128)S(1)}, f32[1,1,128,128]{3,2,1,0:T(8,128)}, u32[]{:S(2)}) copy-start(f32[1,1,128,128]{3,2,1,0:T(8,128)} %param.13) | copy-start | bytes 196612

commit v2 on v1

--- a/solution.py
+++ b/solution.py
@@ -37,8 +37,9 @@
 
 def kernel(
     n_slot, n_tile, n_obs,
-    f_ref, winds_ref, mixing_ref, cells_ref, weights_ref, counts_ref, jac_ref,
+    f_in, winds_in, mixing_in, cells_in, weights_in, counts_in, jac_in,
     state_ref, rad_ref,
+    f_ref, winds_ref, mixing_ref, cells_ref, weights_ref, counts_ref, jac_ref, in_sem,
     ft, halo, packed, edges, rates, coef, gs, gr, w_hi, w_lo, pf, rf, pg, rg,
     halo_send, halo_recv, edge_send, edge_recv, rate_send, rate_recv,
     g_send, g_recv, pf_send, pf_recv, pg_send, pg_recv,
@@ -47,7 +48,7 @@
     tile = lax.axis_index("tile")
     obs = lax.axis_index("obs")
     cx, levels, cy = ft.shape
-    rows = cells_ref.shape[1]
+    rows = cells_ref.shape[2]
     cap = rows // n_obs
     span = cx * 2 * STEPS
     groups = LANES // span
@@ -78,9 +79,12 @@
             halo_send.at[k, c], halo_recv.at[k, c], neighbour(*TILE_DIRS[k]),
         )
 
-    def edge_copy(k, c):
+    edge_parts = (pl.ds(0, 1), pl.ds(1, chunks - 1))
+
+    def edge_copy(k, i):
         return remote(
-            packed.at[c], edges.at[k, c], edge_send.at[k, c], edge_recv.at[k, c], neighbour(*EDGE_DIRS[k])
+            packed.at[edge_parts[i]], edges.at[k, edge_parts[i]],
+            edge_send.at[k, i], edge_recv.at[k, i], neighbour(*EDGE_DIRS[k]),
         )
 
     def rate_copy(k):
@@ -102,12 +106,12 @@
             pg_send.at[by, c], pg_recv.at[by, c], peer(by),
         )
 
-    def each_chunk(body):
+    def each_chunk(body, first=0, last=chunks):
         def step(c, carry):
             body(c)
             return carry
 
-        lax.fori_loop(0, chunks, step, 0)
+        lax.fori_loop(first, last, step, 0)
 
     lane = lax.broadcasted_iota(jnp.int32, (SUB, LANES), 1)
 
@@ -130,10 +134,11 @@
         def one(c):
             for k in range(len(TILE_DIRS)):
                 halo_copy(k, c).start()
+
+        for i, first in enumerate((0, 1)):
             for k in range(len(EDGE_DIRS)):
-                edge_copy(k, c).start()
-
-        each_chunk(one)
+                edge_copy(k, i).start()
+            each_chunk(one, first, chunks if i else 1)
 
     def source_of(x):
         if x < 0:
@@ -142,7 +147,7 @@
             return -1, x - cx
         return 0, x
 
-    def forward():
+    def build_coefs():
         for k in range(len(DIRS)):
             rate_copy(k).wait_recv()
         for x in range(1 - STEPS, cx + STEPS - 1):
@@ -159,6 +164,7 @@
                     coef[x + STEPS, place, 2 * which] = mixing_rate + rate
                     coef[x + STEPS, place, 2 * which + 1] = mixing_rate - rate
 
+    def forward(first, last):
         first_lane = lane == 0
         last_lane = lane == LANES - 1
         lower = lax.rem(lane, 2 * STEPS) < STEPS
@@ -166,8 +172,6 @@
         def one(c):
             for k in range(len(TILE_DIRS)):
                 halo_copy(k, c).wait_recv()
-            for k in range(len(EDGE_DIRS)):
-                edge_copy(k, c).wait_recv()
 
             def group(h, carry):
                 level = pl.ds(pl.multiple_of(c * depth + h * SUB, SUB), SUB)
@@ -218,28 +222,10 @@
             lax.fori_loop(0, groups, group, 0)
             g_copy(c).start()
 
-        each_chunk(one)
-
-    barrier = pltpu.get_barrier_semaphore()
-    greeted = [neighbour(*d) for d in DIRS] + [peer(by) for by in range(1, n_obs)] + [along(1), along(-1)]
-    for to in greeted:
-        pl.semaphore_signal(barrier, inc=1, device_id=to, device_id_type=MESH)
-
-    @pl.when(slot == 0)
-    def _():
-        pack(f_ref)
-
-    pl.semaphore_wait(barrier, len(greeted))
-
-    @pl.when(slot < n_slot - 1)
-    def _():
-        for k in range(len(DIRS)):
-            rate_copy(k).start()
-
-    @pl.when(slot == 0)
-    def _():
-        send_halos()
-        forward()
+        if first < 2:
+            for k in range(len(EDGE_DIRS)):
+                edge_copy(k, first).wait_recv()
+        each_chunk(one, first, last)
 
     tall = cy
     base = lax.broadcasted_iota(jnp.int32, (tall, cap), 0)
@@ -247,9 +233,9 @@
 
     def owner_weights(q, carry):
         cols = pl.ds(pl.multiple_of(q * cap, cap), cap)
-        live = live_row < counts_ref[0, q]
-        cell = [cells_ref[pl.ds(p, 1), cols] for p in range(cells_ref.shape[0])]
-        weight = [jnp.where(live, weights_ref[pl.ds(p, 1), cols], 0.0) for p in range(cells_ref.shape[0])]
+        live = live_row < counts_ref[0, 0, q]
+        cell = [cells_ref[p, :, cols] for p in range(cells_ref.shape[0])]
+        weight = [jnp.where(live, weights_ref[p, :, cols], 0.0) for p in range(cells_ref.shape[0])]
 
         def row_weights(x, inner):
             total = jnp.zeros((tall, cap), jnp.float32)
@@ -264,7 +250,6 @@
         lax.fori_loop(0, cx, row_weights, 0)
         return carry
 
-    lax.fori_loop(0, n_obs, owner_weights, 0)
 
     wide = 2 * cap if n_obs % 2 == 0 else cap
 
@@ -288,9 +273,56 @@
     def keep_pf(q, value):
         pf[q] = value
 
-    interpolate([f_ref[pl.ds(x, levels, stride=cx), :] for x in range(cx)], keep_pf)
+    def interpolate_forcing():
+        lax.fori_loop(0, n_obs, owner_weights, 0)
+        interpolate([f_ref[pl.ds(x, levels, stride=cx), :] for x in range(cx)], keep_pf)
+
+    early = chunks // 2
+
+    barrier = pltpu.get_barrier_semaphore()
+    greeted = [neighbour(*d) for d in DIRS] + [peer(by) for by in range(1, n_obs)] + [along(1), along(-1)]
+    for to in greeted:
+        pl.semaphore_signal(barrier, inc=1, device_id=to, device_id_type=MESH)
+
+    pairs = (
+        (winds_in, winds_ref), (f_in, f_ref), (cells_in, cells_ref), (weights_in, weights_ref),
+        (counts_in, counts_ref), (mixing_in, mixing_ref), (jac_in, jac_ref),
+    )
+    fetches = [pltpu.make_async_copy(src, dst, in_sem.at[i]) for i, (src, dst) in enumerate(pairs)]
+    for fetch in fetches:
+        fetch.start()
+    for fetch in fetches:
+        fetch.wait()
+
+    @pl.when(slot == 0)
+    def _():
+        pack(f_ref)
+
+    @pl.when(slot > 0)
+    def _():
+        interpolate_forcing()
+
+    pl.semaphore_wait(barrier, len(greeted))
+
+    @pl.when(slot < n_slot - 1)
+    def _():
+        for k in range(len(DIRS)):
+            rate_copy(k).start()
+
+    @pl.when(slot == 0)
+    def _():
+        send_halos()
+        build_coefs()
+        forward(0, 1)
+        forward(1, early)
+        interpolate_forcing()
+
     for by in range(1, n_obs):
         pf_copy(by).start()
+
+    @pl.when(slot == 0)
+    def _():
+        forward(early, chunks)
 
     eye = jnp.where(
         lax.broadcasted_iota(jnp.int32, (levels, levels), 0) == lax.broadcasted_iota(jnp.int32, (levels, levels), 1),
@@ -329,7 +361,10 @@
         def _():
             pack(state_ref)
             send_halos()
-            forward()
+            build_coefs()
+            forward(0, 1)
+            forward(1, early)
+            forward(early, chunks)
 
     def owner_out(o, value):
         rad_ref[:, pl.ds(pl.multiple_of(o * cap, cap), cap)] = value
@@ -384,11 +419,23 @@
         def left(c):
             for k in range(len(TILE_DIRS)):
                 halo_copy(k, c).wait_send()
-            for k in range(len(EDGE_DIRS)):
-                edge_copy(k, c).wait_send()
             g_copy(c).wait_send()
 
         each_chunk(left)
+        for k in range(len(EDGE_DIRS)):
+            for i in range(2):
+                edge_copy(k, i).wait_send()
+
+
+def write_out(states, radiances, states_out, radiances_out, sem):
+    copies = [
+        pltpu.make_async_copy(states, states_out, sem.at[0]),
+        pltpu.make_async_copy(radiances, radiances_out, sem.at[1]),
+    ]
+    for copy in copies:
+        copy.start()
+    for copy in copies:
+        copy.wait()
 
 
 def solution(mesh):
@@ -403,15 +450,24 @@
         f32, bf16 = jnp.float32, jnp.bfloat16
         dma = pltpu.SemaphoreType.DMA
         vmem = pl.BlockSpec(memory_space=pltpu.VMEM)
+        hbm = pl.BlockSpec(memory_space=pltpu.HBM)
         states, radiances = pl.pallas_call(
             functools.partial(kernel, n_slot, n_tile, n_obs),
             out_shape=(
                 jax.ShapeDtypeStruct((levels * cx, cy), f32),
                 jax.ShapeDtypeStruct((channels, rows), f32),
             ),
-            in_specs=[vmem] * 5 + [pl.BlockSpec(memory_space=pltpu.SMEM), vmem],
+            in_specs=[hbm] * 7,
             out_specs=(vmem, vmem),
             scratch_shapes=[
+                pltpu.VMEM((levels * cx, cy), f32),
+                pltpu.VMEM((2, cx, cy), f32),
+                pltpu.VMEM(mixing.shape, f32),
+                pltpu.VMEM(observation_columns.shape, jnp.int32),
+                pltpu.VMEM(obs_weights.shape, f32),
+                pltpu.SMEM(obs_counts.shape, jnp.int32),
+                pltpu.VMEM((channels, levels), f32),
+                dma((7,)),
                 pltpu.VMEM((cx, levels, cy), f32),
                 pltpu.VMEM((2, STEPS, levels, cy), f32),
                 pltpu.VMEM((chunks, SUB, LANES), f32),
@@ -427,7 +483,7 @@
                 pltpu.VMEM((n_obs, levels, cap), f32),
                 pltpu.VMEM((n_obs, levels, cap), f32),
                 dma((2, chunks)), dma((2, chunks)),
-                dma((len(EDGE_DIRS), chunks)), dma((len(EDGE_DIRS), chunks)),
+                dma((len(EDGE_DIRS), 2)), dma((len(EDGE_DIRS), 2)),
                 dma((len(DIRS),)), dma((len(DIRS),)),
                 dma((chunks,)), dma((chunks,)),
                 dma((n_obs,)), dma((n_obs,)),
@@ -436,15 +492,26 @@
             compiler_params=pltpu.CompilerParams(
                 collective_id=0, has_side_effects=True, vmem_limit_bytes=48 * 1024 * 1024
             ),
-        )(
+        )(*(pltpu.with_memory_space_constraint(v, pltpu.HBM) for v in (
             forcing.reshape(levels * cx, cy),
             winds.reshape(2, cx, cy),
             mixing,
-            observation_columns.reshape(-1, rows),
-            obs_weights.reshape(-1, rows),
-            obs_counts.reshape(1, n_obs),
+            observation_columns,
+            obs_weights,
+            obs_counts,
             jacobian.reshape(channels, levels),
-        )
+        )))
+        states, radiances = pl.pallas_call(
+            write_out,
+            out_shape=(
+                jax.ShapeDtypeStruct((levels * cx, cy), f32),
+                jax.ShapeDtypeStruct((channels, rows), f32),
+            ),
+            in_specs=[vmem, vmem],
+            out_specs=(hbm, hbm),
+            scratch_shapes=[dma((2,))],
+            compiler_params=pltpu.CompilerParams(vmem_limit_bytes=2 * 1024 * 1024),
+        )(states, radiances)
         return states.reshape(1, levels, cx, cy), radiances.reshape(1, channels, rows)
 
     return jax.shard_map(

time: 40.1 us -> 34.3 us (0.86)
  the two profiles are of different devices: /device:TPU:1 before, /device:TPU:3 now
where the time goes in v2:
time: 34.3 us; the launch traced here: 34.1 us
  Pallas kernels  33.5 us (98%)
  between operations  0.64 us (2%)
    pallas_call x1, Pallas kernels, local(): pl.pallas_call(functools.partial(kernel, n_slot, n_tile, n_obs), out_shap...  32.6 us
    pallas_call x1, Pallas kernels, local(): pl.pallas_call(write_out, out_shape=(jax.ShapeDtypeStruct((levels * cx, c...  0.89 us

profile of v2, /device:TPU:3, one launch (start us, length us, event | category | flops | bytes accessed | tf_op | source)
XLA Modules:
  0.0 34.1 jit_solution(3526727461998443110)
XLA Ops:
  0.6 32.6 %shard_map.86 = (f32[1024,128]{1,0:T(8,128)S(1)}, f32[128,512]{1,0:T(8,128)S(1)}) custom-call(f32[1024,128]{1,0:T(8,128)} %bitcast.5, f32[2,8,128]{2,1,0:T(8,128)} %bitcast.7, f32[128,128]{1,0:T(8,128)} %mixing_in.1, s32[4,1,512]{2,1,0:T(1,128)} %cells_in.1, f32[4,1,512]{2,1,0:T(1,128)} %weights_in.1, s32[1,1,4]{2,1,0:T(1,128)} %counts_in.1, f32[128,128]{1,0:T(8,128)} %bitcast.6), custom_call_target="tpu_custom_call" | custom-call | tf_op jit(solution)/shard_map/pallas_call | solution.py:454
  33.2 0.9 %shard_map.87 = (f32[1024,128]{1,0:T(8,128)}, f32[128,512]{1,0:T(8,128)}) custom-call(f32[1024,128]{1,0:T(8,128)S(1)} %get-tuple-element.6.states, f32[128,512]{1,0:T(8,128)S(1)} %get-tuple-element.7.radiances), custom_call_target="tpu_custom_call" | custom-call | tf_op jit(solution)/shard_map/pallas_call | solution.py:504

commit v3 on v2

--- a/solution.py
+++ b/solution.py
@@ -39,7 +39,7 @@
     n_slot, n_tile, n_obs,
     f_in, winds_in, mixing_in, cells_in, weights_in, counts_in, jac_in,
     state_ref, rad_ref,
-    f_ref, winds_ref, mixing_ref, cells_ref, weights_ref, counts_ref, jac_ref, in_sem,
+    f_ref, winds_ref, mixing_ref, cells_ref, weights_ref, counts_ref, jac_ref, in_sem, table_hi, table_lo,
     ft, halo, packed, edges, rates, coef, gs, gr, w_hi, w_lo, pf, rf, pg, rg,
     halo_send, halo_recv, edge_send, edge_recv, rate_send, rate_recv,
     g_send, g_recv, pf_send, pf_recv, pg_send, pg_recv,
@@ -277,8 +277,6 @@
         lax.fori_loop(0, n_obs, owner_weights, 0)
         interpolate([f_ref[pl.ds(x, levels, stride=cx), :] for x in range(cx)], keep_pf)
 
-    early = chunks // 2
-
     barrier = pltpu.get_barrier_semaphore()
     greeted = [neighbour(*d) for d in DIRS] + [peer(by) for by in range(1, n_obs)] + [along(1), along(-1)]
     for to in greeted:
@@ -314,15 +312,11 @@
         send_halos()
         build_coefs()
         forward(0, 1)
-        forward(1, early)
+        forward(1, chunks)
         interpolate_forcing()
 
     for by in range(1, n_obs):
         pf_copy(by).start()
-
-    @pl.when(slot == 0)
-    def _():
-        forward(early, chunks)
 
     eye = jnp.where(
         lax.broadcasted_iota(jnp.int32, (levels, levels), 0) == lax.broadcasted_iota(jnp.int32, (levels, levels), 1),
@@ -335,6 +329,10 @@
 
     @pl.when(slot > 0)
     def _():
+        table_hi[...], table_lo[...] = halves(jnp.concatenate([jac, exact(jac, power)], axis=1))
+
+    @pl.when(slot > 0)
+    def _():
         def one(c):
             g_copy(c).wait_recv()
 
@@ -363,8 +361,7 @@
             send_halos()
             build_coefs()
             forward(0, 1)
-            forward(1, early)
-            forward(early, chunks)
+            forward(1, chunks)
 
     def owner_out(o, value):
         rad_ref[:, pl.ds(pl.multiple_of(o * cap, cap), cap)] = value
@@ -382,7 +379,7 @@
                 pg_copy(by, c).wait_recv()
 
         each_chunk(arrived)
-        table = halves(jnp.concatenate([jac, exact(jac, power)], axis=1))
+        table = (table_hi[...], table_lo[...])
 
         def one(o, carry):
             owner_out(o, dot3(table, halves(jnp.concatenate([rf[o], rg[o]], axis=0))))
@@ -468,6 +465,8 @@
                 pltpu.SMEM(obs_counts.shape, jnp.int32),
                 pltpu.VMEM((channels, levels), f32),
                 dma((7,)),
+                pltpu.VMEM((channels, 2 * levels), bf16),
+                pltpu.VMEM((channels, 2 * levels), bf16),
                 pltpu.VMEM((cx, levels, cy), f32),
                 pltpu.VMEM((2, STEPS, levels, cy), f32),
                 pltpu.VMEM((chunks, SUB, LANES), f32),

time: 34.3 us -> 33.6 us (0.980)
  the two profiles are of different devices: /device:TPU:3 before, /device:TPU:1 now
where the time goes in v3:
time: 33.6 us; the launch traced here: 33.4 us
  Pallas kernels  32.7 us (97%)
  between operations  0.64 us (2%)
    pallas_call x1, Pallas kernels, local(): pl.pallas_call(functools.partial(kernel, n_slot, n_tile, n_obs), out_shap...  31.9 us
    pallas_call x1, Pallas kernels, local(): pl.pallas_call(write_out, out_shape=(jax.ShapeDtypeStruct((levels * cx, c...  0.89 us

profile of v3, /device:TPU:1, one launch (start us, length us, event | category | flops | bytes accessed | tf_op | source)
XLA Modules:
  0.0 33.4 jit_solution(4134868280131730937)
XLA Ops:
  0.6 31.9 %shard_map.86 = (f32[1024,128]{1,0:T(8,128)S(1)}, f32[128,512]{1,0:T(8,128)S(1)}) custom-call(f32[1024,128]{1,0:T(8,128)} %bitcast.5, f32[2,8,128]{2,1,0:T(8,128)} %bitcast.7, f32[128,128]{1,0:T(8,128)} %mixing_in.1, s32[4,1,512]{2,1,0:T(1,128)} %cells_in.1, f32[4,1,512]{2,1,0:T(1,128)} %weights_in.1, s32[1,1,4]{2,1,0:T(1,128)} %counts_in.1, f32[128,128]{1,0:T(8,128)} %bitcast.6), custom_call_target="tpu_custom_call" | custom-call | tf_op jit(solution)/shard_map/pallas_call | solution.py:451
  32.5 0.9 %shard_map.87 = (f32[1024,128]{1,0:T(8,128)}, f32[128,512]{1,0:T(8,128)}) custom-call(f32[1024,128]{1,0:T(8,128)S(1)} %get-tuple-element.6.states, f32[128,512]{1,0:T(8,128)S(1)} %get-tuple-element.7.radiances), custom_call_target="tpu_custom_call" | custom-call | tf_op jit(solution)/shard_map/pallas_call | solution.py:503
